TPU v7x, 32 devices: a whole 2x2x4 slice. The times are simulated.
32 devices in a mesh: grp: 2 (over x), seq: 16 (over z, y, core).
Axes of the slice: x: 2, y: 2, z: 4, core: 2. Of those that a mesh axis runs over, the one named last changes fastest.
Arguments:
- query_vectors: bfloat16 [4096, 4096], P(('grp', 'seq')), parts along dimension 0, may hold values from -0.5 to 0.5
- key_vectors: bfloat16 [4096, 4096], P(('grp', 'seq')), parts along dimension 0, may hold values from -0.5 to 0.5
- value_vectors: bfloat16 [4096, 2048], P(('grp', 'seq')), parts along dimension 0, may hold values from -6 to 6
- level_weights: bfloat16 [12, 32, 4096], P(None, None, ('grp', 'seq')), parts along dimension 2, may hold values from 0.049804688 to 0.5
Outputs:
- attended: bfloat16 [4096, 2048], P(('grp', 'seq')), parts along dimension 0
There are 2 independent parts, one for each index of `grp`. A program takes and returns all parts, laid end to end along the dimension named above; each array names one. Nothing has to cross between parts.
All inputs are finite; a program needn't handle non-finite values.
Results may differ from a plain program's by a relative error of at most 0.0019.
Values sent between devices are 32-bit elements; how exact they have to be, the bound alone decides.
A program may use at most 64 MiB of HBM per device.

v0:
```python
import jax
import jax.numpy as jnp
from jax import lax
from jax.sharding import PartitionSpec as P


def from_partner(block, axis, apart):
    count = lax.axis_size(axis)
    route = []
    for low in range(count):
        high = low | 1 << apart
        if high != low and high < count:
            route += [(low, high), (high, low)]
    return lax.ppermute(block, axis, route)


def local_onehot(tok_count, local_levels):
    query_pos = lax.broadcasted_iota(jnp.int32, (tok_count, tok_count), 0)
    key_pos = lax.broadcasted_iota(jnp.int32, (tok_count, tok_count), 1)
    depth_map = jnp.zeros((tok_count, tok_count), jnp.int32)
    for shift_bits in range(local_levels - 1):
        differs = jnp.right_shift(query_pos, shift_bits) != jnp.right_shift(key_pos, shift_bits)
        depth_map = depth_map + differs.astype(jnp.int32)
    causal = key_pos <= query_pos
    level_ids = lax.broadcasted_iota(jnp.int32, (local_levels, tok_count, tok_count), 0)
    chosen = (level_ids == depth_map[None]) & causal[None]
    return jnp.where(chosen, 1.0, 0.0).astype(jnp.bfloat16)


def on_device(query_vectors, key_vectors, value_vectors, level_weights):
    tok_count = query_vectors.shape[0]
    head_count = level_weights.shape[1]
    state_width = query_vectors.shape[1] // head_count
    value_width = value_vectors.shape[1] // head_count
    query_heads = query_vectors.reshape(tok_count, head_count, state_width)
    key_heads = key_vectors.reshape(tok_count, head_count, state_width)
    value_heads = value_vectors.reshape(tok_count, head_count, value_width)
    local_levels = tok_count.bit_length()
    seq_bits = lax.axis_size("seq").bit_length() - 1
    position = lax.axis_index("seq")
    states = jnp.einsum("tgn,tgp->gnp", key_heads, value_heads, preferred_element_type=jnp.float32)
    levels = []
    totals = states
    for bit_index in range(seq_bits):
        partner = from_partner(totals, "seq", bit_index)
        upper_half = jnp.right_shift(position, bit_index) % 2 == 1
        levels.append(jnp.where(upper_half, partner, 0.0))
        totals = totals + partner
    onehot = local_onehot(tok_count, local_levels)
    group_width = min(8, head_count)
    pieces = []
    for head_start in range(0, head_count, group_width):
        head_stop = head_start + group_width
        query_group = query_heads[:, head_start:head_stop]
        key_group = key_heads[:, head_start:head_stop]
        value_group = value_heads[:, head_start:head_stop]
        lam_group = level_weights[:local_levels, head_start:head_stop]
        scores = jnp.einsum(
            "tgn,sgn->gts", query_group, key_group, preferred_element_type=jnp.float32
        )
        mixing = jnp.einsum("lgt,lts->gts", lam_group, onehot, preferred_element_type=jnp.float32)
        weights = (mixing * scores).astype(jnp.bfloat16)
        pieces.append(
            jnp.einsum("gts,sgp->tgp", weights, value_group, preferred_element_type=jnp.float32)
        )
    local_term = jnp.concatenate(pieces, axis=1)
    query_wide = query_heads.astype(jnp.float32)
    cross_term = jnp.zeros((tok_count, head_count, value_width), jnp.float32)
    for bit_index in range(seq_bits):
        lam_row = level_weights[local_levels + bit_index].astype(jnp.float32).T
        product = jnp.einsum(
            "thn,hnp->thp", query_wide, levels[bit_index], precision=lax.Precision.HIGHEST
        )
        cross_term = cross_term + lam_row[:, :, None] * product
    attended = (local_term + cross_term).astype(jnp.bfloat16)
    return attended.reshape(tok_count, head_count * value_width)


def solution(mesh):
    placed = (
        P(("grp", "seq"), None),
        P(("grp", "seq"), None),
        P(("grp", "seq"), None),
        P(None, None, ("grp", "seq")),
    )
    return jax.shard_map(
        on_device, mesh=mesh, in_specs=placed, out_specs=P(("grp", "seq"), None), check_vma=False
    )
```

profile of v0, /device:TPU:25, one launch (start us, length us, event | category | flops | bytes accessed | tf_op | source)
XLA Modules:
  0.0 113.3 jit_solution(6262472694564194436)
XLA Ops:
  0.0 1.4 %copy.5 = bf16[128,2048]{0,1:T(8,128)(2,1)S(1)} copy(bf16[128,2048]{1,0:T(8,128)(2,1)} %param.6) | data formatting | bytes 1048576 | tf_op args[2]
  2.8 2.0 %collective-permute-done = f32[32,128,64]{1,2,0:T(8,128)S(1)} collective-permute-done((f32[32,128,64]{1,2,0:T(8,128)S(1)}, f32[32,128,64]{1,2,0:T(8,128)S(1)}, u32[]{:S(2)}, u32[]{:S(2)}) %collective-permute-start) | collective-permute-done | bytes 1048608 | tf_op jit(solution)/shard_map/ppermute | solution.py:14
  5.9 1.2 %collective-permute-start.1 = (f32[32,128,64]{1,2,0:T(8,128)S(1)}, f32[32,128,64]{1,2,0:T(8,128)}, u32[]{:S(2)}, u32[]{:S(2)}) collective-permute-start(f32[32,128,64]{1,2,0:T(8,128)S(1)} %add.120), channel_id=1, source_target_pairs={{0,2},{2,0},{1,3},{3,1},{4,6},{6,4},{5,7},{7,5},{8,10},{10,8},{9,1... | collective-permute-start | bytes 3145736 | tf_op jit(solution)/shard_map/ppermute | solution.py:14
  7.3 0.9 copy.25
  9.3 1.0 copy-done.4
  10.7 1.1 %fusion.67 = f32[128,128,8]{1,2,0:T(8,128)} fusion(bf16[8,8,128]{1,0,2:T(8,128)(2,1)S(1)} %copy.13, bf16[8,128,128]{2,1,0:T(8,128)(2,1)S(1)} %select_convert_fusion), kind=kOutput, calls=%fused_computation.73 | convolution fusion | flops 2097152 | bytes 802816 | tf_op jit(solution)/shard_map/lgt,lts->gts/dot_general | solution.py:61
  12.2 1.4 %fusion.77 = (bf16[128,8,128]{2,1,0:T(8,128)(2,1)}, bf16[128,8,128]{2,1,0:T(8,128)(2,1)}, bf16[128,8,128]{2,1,0:T(8,128)(2,1)}, bf16[128,8,128]{2,1,0:T(8,128)(2...) fusion(bf16[128,32,128]{2,1,0:T(8,128)(2,1)S(1)} %bitcast.121, ...), kind=kLoop, calls=%fused_computation.96 | loop fusion | bytes 4194304 | tf_op jit(solution)/shard_map/slice | solution.py:54
  13.6 16.7 %collective-permute-done.1 = f32[32,128,64]{1,2,0:T(8,128)} collective-permute-done((f32[32,128,64]{1,2,0:T(8,128)S(1)}, f32[32,128,64]{1,2,0:T(8,128)}, u32[]{:S(2)}, u32[]{:S(2)}) %collective-permute-start.1) | collective-permute-done | bytes 1048608 | tf_op jit(solution)/shard_map/ppermute | solution.py:14
  30.3 1.4 %add.123 = f32[32,128,64]{1,2,0:T(8,128)S(1)} add(f32[32,128,64]{1,2,0:T(8,128)S(1)} %copy-done.2, f32[32,128,64]{1,2,0:T(8,128)} %collective-permute-done.1) | non-fusion elementwise | flops 262144 | bytes 3145728 | tf_op jit(solution)/shard_map/add | solution.py:48
  32.0 1.1 %fusion.63 = f32[128,128,8]{1,2,0:T(8,128)} fusion(bf16[8,8,128]{1,0,2:T(8,128)(2,1)S(1)} %copy-done.13, bf16[8,128,128]{2,1,0:T(8,128)(2,1)S(1)} %select_convert_fusion), kind=kOutput, calls=%fused_computation.69 | convolution fusion | flops 2097152 | bytes 802816 | tf_op jit(solution)/shard_map/lgt,lts->gts/dot_general | solution.py:61
  33.1 0.9 copy.17
  34.0 2.1 %fusion.65 = f32[128,128,8]{1,2,0:T(8,128)} fusion(bf16[8,8,128]{1,0,2:T(8,128)(2,1)} %copy.17, bf16[8,128,128]{2,1,0:T(8,128)(2,1)S(1)} %select_convert_fusion), kind=kOutput, calls=%fused_computation.71 | convolution fusion | flops 2097152 | bytes 802816 | tf_op jit(solution)/shard_map/lgt,lts->gts/dot_general | solution.py:61
  36.0 2.4 %convolution_bitcast_fusion.6 = f32[128,8,64]{0,2,1:T(8,128)} fusion(f32[128,128,8]{1,2,0:T(8,128)} %fusion.65, bf16[128,8,128]{2,1,0:T(8,128)(2,1)} %get-tuple-element.27, bf16[128,8,128]{2,1,0:T(8,128)(2,1)} %get-tuple-element.8, bf16[128,32,64]{0,2,1:T(8,128)(2,1)S(1)} %bitcast.116), kind=kOutput, calls=%fused_computation.23 | convolution fusion | flops 50593792 | bytes 1441792 | tf_op jit(solution)/shard_map/gts,sgp->tgp/dot_general | solution.py:64
  38.4 2.4 %convolution_bitcast_fusion.5 = f32[128,8,64]{0,2,1:T(8,128)} fusion(f32[128,128,8]{1,2,0:T(8,128)} %fusion.63, bf16[128,8,128]{2,1,0:T(8,128)(2,1)} %get-tuple-element.28, bf16[128,8,128]{2,1,0:T(8,128)(2,1)} %get-tuple-element.7, bf16[128,32,64]{0,2,1:T(8,128)(2,1)S(1)} %bitcast.117), kind=kOutput, calls=%fused_computation.22 | convolution fusion | flops 50593792 | bytes 1441792 | tf_op jit(solution)/shard_map/gts,sgp->tgp/dot_general | solution.py:64
  40.9 2.3 %convolution_bitcast_fusion.7 = f32[128,8,64]{0,2,1:T(8,128)} fusion(f32[128,128,8]{1,2,0:T(8,128)} %fusion.67, bf16[128,8,128]{2,1,0:T(8,128)(2,1)} %get-tuple-element.30, bf16[128,8,128]{2,1,0:T(8,128)(2,1)S(1)} %copy-done.8, bf16[128,32,64]{0,2,1:T(8,128)(2,1)S(1)} %bitcast.118), kind=kOutput, calls=%fused_computation.24 | convolution fusion | flops 50593792 | bytes 1441792 | tf_op jit(solution)/shard_map/gts,sgp->tgp/dot_general | solution.py:64
  43.2 12.2 %collective-permute-done.2 = f32[32,128,64]{1,2,0:T(8,128)} collective-permute-done((f32[32,128,64]{1,2,0:T(8,128)S(1)}, f32[32,128,64]{1,2,0:T(8,128)}, u32[]{:S(2)}, u32[]{:S(2)}) %collective-permute-start.2) | collective-permute-done | bytes 1048608 | tf_op jit(solution)/shard_map/ppermute | solution.py:14
  55.4 2.4 %add.126 = f32[32,128,64]{1,2,0:T(8,128)} add(f32[32,128,64]{1,2,0:T(8,128)S(1)} %add.123, f32[32,128,64]{1,2,0:T(8,128)} %collective-permute-done.2) | non-fusion elementwise | flops 262144 | bytes 3145728 | tf_op jit(solution)/shard_map/add | solution.py:48
  57.9 2.1 %convolution_bitcast_fusion.4 = f32[128,8,64]{0,2,1:T(8,128)} fusion(f32[128,128,8]{1,2,0:T(8,128)S(1)} %fusion.61, bf16[128,8,128]{2,1,0:T(8,128)(2,1)} %get-tuple-element.29, bf16[128,8,128]{2,1,0:T(8,128)(2,1)S(1)} %copy-done.7, bf16[128,32,64]{0,2,1:T(8,128)(2,1)S(1)} %bitcast.119), kind=kOutput, calls=%fused_computation.21 | convolution fusion | flops 50593792 | bytes 1441792 | tf_op jit(solution)/shard_map/gts,sgp->tgp/dot_general | solution.py:64
  60.0 2.2 %fusion.2 = f32[128,32,64]{0,2,1:T(8,128)S(1)} fusion(f32[32,128,64]{1,2,0:T(8,128)} %collective-permute-done.1, f32[128,32]{0,1:T(8,128)S(1)} %get-tuple-element.14, pred[]{:T(512)S(6)} %eq.40, bf16[128,4096]{1,0:T(8,128)(2,1)S(1)} %copy-done), kind=kOutput, calls=%fused_computation.5 | convolution fusion | flops 403177472 | bytes 3162113 | tf_op jit(solution)/shard_map/thn,hnp->thp/dot_general | solution.py:71
  62.2 3.4 %fusion.1 = f32[128,32,64]{0,2,1:T(8,128)S(1)} fusion(f32[32,128,64]{1,2,0:T(8,128)} %collective-permute-done.2, f32[128,32]{0,1:T(8,128)S(1)} %get-tuple-element.16, pred[]{:T(512)S(6)} %eq.41, bf16[128,4096]{1,0:T(8,128)(2,1)S(1)} %copy-done), kind=kOutput, calls=%fused_computation.3 | convolution fusion | flops 403177472 | bytes 3162113 | tf_op jit(solution)/shard_map/thn,hnp->thp/dot_general | solution.py:71
  65.6 40.9 %collective-permute-done.3 = f32[32,128,64]{1,2,0:T(8,128)} collective-permute-done((f32[32,128,64]{1,2,0:T(8,128)}, f32[32,128,64]{1,2,0:T(8,128)}, u32[]{:S(2)}, u32[]{:S(2)}) %collective-permute-start.3) | collective-permute-done | bytes 1048608 | tf_op jit(solution)/shard_map/ppermute | solution.py:14
  106.5 3.5 %fusion = f32[128,32,64]{0,2,1:T(8,128)S(1)} fusion(f32[32,128,64]{1,2,0:T(8,128)} %collective-permute-done.3, f32[128,32]{0,1:T(8,128)S(1)} %get-tuple-element.15, pred[]{:T(512)S(6)} %eq.42, bf16[128,4096]{1,0:T(8,128)(2,1)S(1)} %copy-done), kind=kOutput, calls=%fused_computation.1 | convolution fusion | flops 403177472 | bytes 3162113 | tf_op jit(solution)/shard_map/thn,hnp->thp/dot_general | solution.py:71
  110.1 2.2 %fusion.8 = bf16[128,32,64]{0,2,1:T(8,128)(2,1)S(1)} fusion(f32[128,32,64]{0,2,1:T(8,128)S(1)} %fusion, f32[128,32,64]{0,2,1:T(8,128)S(1)} %fusion.1, f32[128,32,64]{0,2,1:T(8,128)S(1)} %fusion.2, f32[128,8,64]{0,2,1:T(8,128)S(1)} %copy-done.12, f32[128,8,64]{0,2,1:T(8,128)S(1)} %copy-done.10, f32[128,8,64]{0,2,1:T(8,128)S(1)} %copy-done.9, ...), kind=kOutput, calls=%fused_computation.12 | convolution fusion | flops 405274624 | bytes 6832129 | tf_op jit(solution)/shard_map/thn,hnp->thp/dot_general | solution.py:71
  112.3 1.0 copy.11
  (50 shorter events, 4.7 us)
Async XLA Ops:
  0.0 1.4 %copy-start.3 = (bf16[128,4096]{1,0:T(8,128)(2,1)S(1)}, bf16[128,4096]{1,0:T(8,128)(2,1)}, u32[]{:S(2)}) copy-start(bf16[128,4096]{1,0:T(8,128)(2,1)} %param.5) | copy-start | bytes 3145732
  1.4 1.4 %copy-start.15 = (bf16[12,32,128]{2,1,0:T(8,128)(2,1)S(1)}, bf16[12,32,128]{2,1,0:T(8,128)(2,1)}, u32[]{:S(2)}) copy-start(bf16[12,32,128]{2,1,0:T(8,128)(2,1)} %param.7) | copy-start | bytes 294916
  1.8 3.0 %collective-permute-start = (f32[32,128,64]{1,2,0:T(8,128)S(1)}, f32[32,128,64]{1,2,0:T(8,128)S(1)}, u32[]{:S(2)}, u32[]{:S(2)}) collective-permute-start(f32[32,128,64]{1,2,0:T(8,128)S(1)} %fusion.17), channel_id=1, source_target_pairs={{0,1},{1,0},{2,3},{3,2},{4,5},{5,4},{6,7},{7,6},{8,9},{9,8},{10,11... | collective-permute-start | bytes 3145736 | tf_op jit(solution)/shard_map/ppermute | solution.py:14
  4.9 1.0 copy-start.5
  4.9 4.2 %copy-start = (bf16[128,4096]{1,0:T(8,128)(2,1)S(1)}, bf16[128,4096]{1,0:T(8,128)(2,1)}, u32[]{:S(2)}) copy-start(bf16[128,4096]{1,0:T(8,128)(2,1)} %param.4) | copy-start | bytes 3145732
  5.9 3.5 %copy-start.1 = (f32[32,128,64]{1,2,0:T(8,128)}, f32[32,128,64]{1,2,0:T(8,128)S(1)}, u32[]{:S(2)}) copy-start(f32[32,128,64]{1,2,0:T(8,128)S(1)} %add.120) | copy-start | bytes 3145732
  5.9 24.5 %collective-permute-start.1 = (f32[32,128,64]{1,2,0:T(8,128)S(1)}, f32[32,128,64]{1,2,0:T(8,128)}, u32[]{:S(2)}, u32[]{:S(2)}) collective-permute-start(f32[32,128,64]{1,2,0:T(8,128)S(1)} %add.120), channel_id=1, source_target_pairs={{0,2},{2,0},{1,3},{3,1},{4,6},{6,4},{5,7},{7,5},{8,10},{10,8},{9,1... | collective-permute-start | bytes 3145736 | tf_op jit(solution)/shard_map/ppermute | solution.py:14
  9.1 1.2 %copy-start.4 = (bf16[128,4096]{1,0:T(8,128)(2,1)S(1)}, bf16[128,4096]{1,0:T(8,128)(2,1)}, u32[]{:S(2)}) copy-start(bf16[128,4096]{1,0:T(8,128)(2,1)} %param.5) | copy-start | bytes 3145732
  10.7 1.2 %copy-start.14 = (bf16[8,8,128]{1,0,2:T(8,128)(2,1)S(1)}, bf16[8,8,128]{1,0,2:T(8,128)(2,1)}, u32[]{:S(2)}) copy-start(bf16[8,8,128]{1,0,2:T(8,128)(2,1)} %copy.25) | copy-start | bytes 49156
  12.2 18.2 %copy-start.2 = (f32[32,128,64]{1,2,0:T(8,128)S(1)}, f32[32,128,64]{1,2,0:T(8,128)}, u32[]{:S(2)}) copy-start(f32[32,128,64]{1,2,0:T(8,128)} %copy-done.1) | copy-start | bytes 3145732
  13.6 18.4 %copy-start.13 = (bf16[8,8,128]{1,0,2:T(8,128)(2,1)S(1)}, bf16[8,8,128]{1,0,2:T(8,128)(2,1)}, u32[]{:S(2)}) copy-start(bf16[8,8,128]{1,0,2:T(8,128)(2,1)} %copy.21) | copy-start | bytes 49156
  31.7 23.7 %collective-permute-start.2 = (f32[32,128,64]{1,2,0:T(8,128)S(1)}, f32[32,128,64]{1,2,0:T(8,128)}, u32[]{:S(2)}, u32[]{:S(2)}) collective-permute-start(f32[32,128,64]{1,2,0:T(8,128)S(1)} %add.123), channel_id=1, source_target_pairs={{0,4},{4,0},{1,5},{5,1},{2,6},{6,2},{3,7},{7,3},{8,12},{12,8},{9,1... | collective-permute-start | bytes 3145736 | tf_op jit(solution)/shard_map/ppermute | solution.py:14
  38.4 2.4 %copy-start.8 = (bf16[128,8,128]{2,1,0:T(8,128)(2,1)S(1)}, bf16[128,8,128]{2,1,0:T(8,128)(2,1)}, u32[]{:S(2)}) copy-start(bf16[128,8,128]{2,1,0:T(8,128)(2,1)} %get-tuple-element.5) | copy-start | bytes 786436
  55.4 2.5 %copy-start.7 = (bf16[128,8,128]{2,1,0:T(8,128)(2,1)S(1)}, bf16[128,8,128]{2,1,0:T(8,128)(2,1)}, u32[]{:S(2)}) copy-start(bf16[128,8,128]{2,1,0:T(8,128)(2,1)} %get-tuple-element.6) | copy-start | bytes 786436
  57.8 48.7 %collective-permute-start.3 = (f32[32,128,64]{1,2,0:T(8,128)}, f32[32,128,64]{1,2,0:T(8,128)}, u32[]{:S(2)}, u32[]{:S(2)}) collective-permute-start(f32[32,128,64]{1,2,0:T(8,128)} %add.126), channel_id=1, source_target_pairs={{0,8},{8,0},{1,9},{9,1},{2,10},{10,2},{3,11},{11,3},{4,12},{12,4},... | collective-permute-start | bytes 3145736 | tf_op jit(solution)/shard_map/ppermute | solution.py:14
  106.4 3.6 %copy-start.6 = (f32[32,128,64]{1,2,0:T(8,128)S(1)}, f32[32,128,64]{1,2,0:T(8,128)}, u32[]{:S(2)}) copy-start(f32[32,128,64]{1,2,0:T(8,128)} %copy-done.5) | copy-start | bytes 3145732
  106.5 3.6 %copy-start.9 = (f32[128,8,64]{0,2,1:T(8,128)S(1)}, f32[128,8,64]{0,2,1:T(8,128)}, u32[]{:S(2)}) copy-start(f32[128,8,64]{0,2,1:T(8,128)} %convolution_bitcast_fusion.6) | copy-start | bytes 786436
  106.5 3.6 %copy-start.10 = (f32[128,8,64]{0,2,1:T(8,128)S(1)}, f32[128,8,64]{0,2,1:T(8,128)}, u32[]{:S(2)}) copy-start(f32[128,8,64]{0,2,1:T(8,128)} %convolution_bitcast_fusion.5) | copy-start | bytes 786436
  106.5 3.6 %copy-start.11 = (f32[128,8,64]{0,2,1:T(8,128)S(1)}, f32[128,8,64]{0,2,1:T(8,128)}, u32[]{:S(2)}) copy-start(f32[128,8,64]{0,2,1:T(8,128)} %convolution_bitcast_fusion.7) | copy-start | bytes 786436
  106.5 3.6 %copy-start.12 = (f32[128,8,64]{0,2,1:T(8,128)S(1)}, f32[128,8,64]{0,2,1:T(8,128)}, u32[]{:S(2)}) copy-start(f32[128,8,64]{0,2,1:T(8,128)} %convolution_bitcast_fusion.4) | copy-start | bytes 786436
where the time goes:
time: 114 us; the launch traced here: 113 us
  waiting for transfers between devices  71.9 us (63%)
  matrix products  25.7 us (23%)
  local copies, waits for them, and re-layouts  9.03 us (8%)
  other arithmetic  4.28 us (4%)
  starting transfers between devices  2.26 us (2%)
    ppermute x4, waiting for transfers between devices, from_partner(): return lax.ppermute(block, axis, route)  71.9 us
    dot_general x4, matrix products, on_device(): jnp.einsum('thn,hnp->thp', query_wide, levels[bit_index], precision=lax.P...  11.3 us
    dot_general x4, matrix products, on_device(): jnp.einsum('gts,sgp->tgp', weights, value_group, preferred_element_type=j...  9.26 us
    dot_general x4, matrix products, on_device(): jnp.einsum('lgt,lts->gts', lam_group, onehot, preferred_element_type=jnp....  4.69 us
    add x3, other arithmetic, on_device(): totals = totals + partner  3.95 us
    unnamed x35, local copies, waits for them, and re-layouts  3.77 us
    slice x5, local copies, waits for them, and re-layouts, on_device(): lam_group = level_weights[:local_levels, head_start:head_stop]  2.83 us
  transfers between devices with their start and end apart: 4, of which 4 were waited for; matrix products, arithmetic and copies ran while one was open for 22% of the time, Pallas kernels for 0%

commit v1 on v0

v1 whole, which is shorter than its diff:
```python
import functools

import jax
import jax.numpy as jnp
from jax import lax
from jax.experimental import pallas as pl
from jax.experimental.pallas import tpu as pltpu
from jax.sharding import PartitionSpec as P

CHUNKS = 4
MESH = pl.DeviceIdType.MESH
F32 = jnp.float32
BF16 = jnp.bfloat16
NT = (((1,), (1,)), ((), ()))
NN = (((1,), (0,)), ((), ()))


def kernel(dims, q_hbm, k_hbm, v_hbm, lw_hbm, out_hbm, q, k, v, lw, lam, vt, depth, own, totals,
           levels, acc, out, in_sem, out_sem, send_sem, recv_sem):
    tok, heads, width, value, bits, local_levels = dims
    half = heads // 2
    chunks = min(CHUNKS, half // 2)
    per = half // chunks
    rows = per * value
    pos = lax.axis_index("seq")
    core = pos % 2
    other = 1 - core
    last = bits - 1

    def bit(j):
        return (pos // 2 ** j) % 2

    def open_above(j):
        return (pos // 2 ** (j + 1)) != 2 ** (bits - 1 - j) - 1

    def toggled(j):
        return pos + 2 ** j * (1 - 2 * bit(j))

    relay = 2 ** (last - 1)

    barrier = pltpu.get_barrier_semaphore()
    for j in range(last):
        pl.semaphore_signal(barrier, inc=1, device_id={"seq": toggled(j)}, device_id_type=MESH)
    edge_low = (bit(last) == 0) & (bit(last - 1) == 1)
    edge_high = (bit(last) == 1) & (bit(last - 1) == 0)

    @pl.when(edge_low)
    def _():
        pl.semaphore_signal(barrier, inc=1, device_id={"seq": pos + relay}, device_id_type=MESH)

    @pl.when(edge_high)
    def _():
        pl.semaphore_signal(barrier, inc=1, device_id={"seq": pos - relay}, device_id_type=MESH)

    def cols(head, count, size):
        return pl.ds(pl.multiple_of(head * size, size * 2 if count > 1 else size), count * size)

    def first_head(side, i):
        return side * half + i * per

    order = [(other, i) for i in range(chunks)] + [(core, i) for i in range(chunks)]
    loads = []
    for n, (side, i) in enumerate(order):
        head = first_head(side, i)
        kc, vc = cols(head, per, width), cols(head, per, value)
        pair = (pltpu.make_async_copy(k_hbm.at[:, kc], k.at[:, kc], in_sem.at[2 * n]),
                pltpu.make_async_copy(v_hbm.at[:, vc], v.at[:, vc], in_sem.at[2 * n + 1]))
        for copy in pair:
            copy.start()
        loads.append(pair)
    base = 2 * len(order)
    load_q = pltpu.make_async_copy(q_hbm, q, in_sem.at[base])
    load_lw = pltpu.make_async_copy(lw_hbm, lw, in_sem.at[base + 1])
    load_q.start()
    load_lw.start()

    def state_rows(head, count=1):
        return pl.ds(pl.multiple_of(head * value, value), count * value)

    def make_state(n):
        side, i = order[n]
        for copy in loads[n]:
            copy.wait()
        head = first_head(side, i)
        for p in range(0, per, 2):
            block = v[:, cols(head + p, 2, value)]
            turned = block.astype(F32).T.astype(BF16)
            vt[state_rows(head + p, 2), :] = turned
            for s in range(2):
                own[state_rows(head + p + s), :] = lax.dot_general(
                    turned[s * value:(s + 1) * value], k[:, cols(head + p + s, 1, width)], NN,
                    preferred_element_type=F32)

    def piece(side, i):
        return state_rows(first_head(side, i), per)

    def remote(src, dst, slot, i, target):
        n = slot * chunks + i
        return pltpu.make_async_remote_copy(
            src_ref=src, dst_ref=dst, send_sem=send_sem.at[n], recv_sem=recv_sem.at[n],
            device_id={"seq": target}, device_id_type=MESH)

    mate = toggled(0)

    def swap(i):
        return remote(own.at[piece(other, i)], levels.at[0, piece(other, i)], 0, i, mate)

    def swap_in(i):
        return remote(own.at[piece(core, i)], levels.at[0, piece(core, i)], 0, i, mate)

    def extra(i):
        return remote(own.at[piece(core, i)], levels.at[0, piece(core, i)], 1, i, mate)

    def extra_in(i):
        return remote(own.at[piece(other, i)], levels.at[0, piece(other, i)], 1, i, mate)

    def main(j, i):
        target = toggled(j) if j < last else pos + relay
        return remote(totals.at[j - 1, pl.ds(i * rows, rows)], levels.at[j, piece(core, i)], 1 + j, i, target)

    def main_in(j, i):
        return remote(levels.at[j, piece(core, i)], levels.at[j, piece(core, i)], 1 + j, i, mate)

    def pass_on(i):
        return remote(levels.at[last, piece(core, i)], levels.at[last, piece(core, i)], 1 + last, i, pos + relay)

    def forward(j, i):
        return remote(levels.at[j, piece(core, i)], levels.at[j, piece(core, i)], 1 + last + j, i, mate)

    def forward_in(j, i):
        return remote(levels.at[j, piece(other, i)], levels.at[j, piece(other, i)], 1 + last + j, i, mate)

    def sends(j):
        if j == last:
            return edge_low
        up = bit(j) == 0
        return up | open_above(j) if j < last - 1 else up

    def receives(j):
        up = bit(j) == 1
        return up | open_above(j) if j < last - 1 else up

    for n in range(chunks):
        make_state(n)
        if n == 0:
            pl.semaphore_wait(barrier, last + (bit(last) + bit(last - 1)) % 2)
        swap(n).start()

    def event(j, i):
        if j == 0:
            make_state(chunks + i)

            @pl.when(core == 0)
            def _():
                extra(i).start()

            swap_in(i).wait_recv()
            mine = piece(core, i)
            totals[0, pl.ds(i * rows, rows), :] = own[mine, :] + levels[0, mine, :]

            @pl.when(sends(1))
            def _():
                main(1, i).start()
            return

        @pl.when(receives(j))
        def _():
            main_in(j, i).wait_recv()
            if j == last:
                @pl.when(edge_high)
                def _():
                    pass_on(i).start()
            else:
                @pl.when(open_above(j))
                def _():
                    part = pl.ds(i * rows, rows)
                    totals[j, part, :] = totals[j - 1, part, :] + levels[j, piece(core, i), :]

                    @pl.when(sends(j + 1))
                    def _():
                        main(j + 1, i).start()

            @pl.when(bit(j) == 1)
            def _():
                forward(j, i).start()

    def prepare():
        load_lw.wait()
        for level in range(local_levels + bits):
            lam[level] = lw[level].astype(F32)
        key_pos = lax.broadcasted_iota(jnp.int32, (tok, tok), 0)
        query_pos = lax.broadcasted_iota(jnp.int32, (tok, tok), 1)
        level_map = jnp.zeros((tok, tok), jnp.int32)
        for shift in range(local_levels - 1):
            differs = jnp.right_shift(query_pos, shift) != jnp.right_shift(key_pos, shift)
            level_map = level_map + differs.astype(jnp.int32)
        depth[...] = jnp.where(key_pos <= query_pos, level_map, local_levels)
        load_q.wait()

    def local(start, stop):
        @pl.loop(start, stop)
        def _(n):
            head = lax.rem(n + other * half, heads)
            scores = lax.dot_general(k[:, cols(head, 1, width)], q[:, cols(head, 1, width)], NT,
                                     preferred_element_type=F32)
            level_map = depth[...]
            mixing = jnp.zeros((tok, tok), F32)
            for level in range(local_levels):
                mixing = jnp.where(level_map == level, lam[level, pl.ds(head, 1), :], mixing)
            weight = (mixing * scores).astype(BF16)
            acc[state_rows(head), :] = lax.dot_general(vt[state_rows(head), :], weight, NN,
                                                       preferred_element_type=F32)

    def cross(j, side, i):
        @pl.loop(0, per)
        def _(n):
            head = first_head(side, i) + n
            part = levels[j, state_rows(head), :]
            upper = part.astype(BF16)
            lower = (part - upper.astype(F32)).astype(BF16)
            query = q[:, cols(head, 1, width)]
            product = lax.dot_general(jnp.concatenate([upper, lower], axis=1),
                                      jnp.concatenate([query, query], axis=1), NT,
                                      preferred_element_type=F32)
            acc[state_rows(head), :] += lam[local_levels + j, pl.ds(head, 1), :] * product

    def cross_level(j):
        @pl.when(bit(j) == 1)
        def _():
            for i in range(chunks):
                cross(j, core, i)
            for i in range(chunks):
                (extra_in(i) if j == 0 else forward_in(j, i)).wait_recv()
                cross(j, other, i)

    def out_copy(side, i):
        n = i if side is core else chunks + i
        part = cols(first_head(side, i), per, value)
        return pltpu.make_async_copy(out.at[:, part], out_hbm.at[:, part], out_sem.at[n])

    def finish(side, i):
        head = first_head(side, i)
        for p in range(0, per, 2):
            out[:, cols(head + p, 2, value)] = acc[state_rows(head + p, 2), :].T.astype(BF16)
        out_copy(side, i).start()

    steps = chunks + bits - 1
    share = -(-heads // (steps - 2))
    done = 0
    pending = list(range(last))
    for d in range(steps):
        for j in reversed(range(bits)):
            if 0 <= d - j < chunks:
                event(j, d - j)
        if d == 0:
            prepare()
        stop = min(heads, done + share)
        if stop > done:
            local(done, stop)
        done = stop
        if done == heads and d >= steps - last and pending:
            cross_level(pending.pop(0))
    for j in pending:
        cross_level(j)
    for side, receive in ((core, None), (other, forward_in)):
        for i in range(chunks):
            @pl.when(bit(last) == 1)
            def _():
                if receive is not None:
                    receive(last, i).wait_recv()
                cross(last, side, i)
            finish(side, i)

    for i in range(chunks):
        swap(i).wait_send()

        @pl.when(core == 0)
        def _():
            extra(i).wait_send()

        for j in range(1, bits):
            @pl.when(sends(j))
            def _():
                main(j, i).wait_send()

            @pl.when(bit(j) == 1)
            def _():
                forward(j, i).wait_send()

        @pl.when(edge_high)
        def _():
            pass_on(i).wait_send()

        out_copy(core, i).wait()
        out_copy(other, i).wait()


def on_device(query_vectors, key_vectors, value_vectors, level_weights):
    tok = query_vectors.shape[0]
    level_count, heads, _ = level_weights.shape
    width = query_vectors.shape[1] // heads
    value = value_vectors.shape[1] // heads
    bits = lax.axis_size("seq").bit_length() - 1
    local_levels = tok.bit_length()
    chunks = min(CHUNKS, heads // 4)
    slots = (1 + 2 * bits) * chunks
    anywhere = pl.BlockSpec(memory_space=pl.ANY)
    return pl.pallas_call(
        functools.partial(kernel, (tok, heads, width, value, bits, local_levels)),
        out_shape=jax.ShapeDtypeStruct((tok, heads * value), BF16),
        in_specs=[anywhere] * 4,
        out_specs=anywhere,
        scratch_shapes=[
            pltpu.VMEM(query_vectors.shape, BF16),
            pltpu.VMEM(key_vectors.shape, BF16),
            pltpu.VMEM(value_vectors.shape, BF16),
            pltpu.VMEM(level_weights.shape, BF16),
            pltpu.VMEM(level_weights.shape, F32),
            pltpu.VMEM((heads * value, tok), BF16),
            pltpu.VMEM((tok, tok), jnp.int32),
            pltpu.VMEM((heads * value, width), F32),
            pltpu.VMEM((bits - 1, heads * value // 2, width), F32),
            pltpu.VMEM((bits, heads * value, width), F32),
            pltpu.VMEM((heads * value, tok), F32),
            pltpu.VMEM((tok, heads * value), BF16),
            pltpu.SemaphoreType.DMA((4 * chunks + 2,)),
            pltpu.SemaphoreType.DMA((2 * chunks,)),
            pltpu.SemaphoreType.DMA((slots,)),
            pltpu.SemaphoreType.DMA((slots,)),
        ],
        compiler_params=pltpu.CompilerParams(collective_id=0, has_side_effects=True),
    )(query_vectors, key_vectors, value_vectors, level_weights)


def solution(mesh):
    rows = P(("grp", "seq"), None)
    placed = (rows, rows, rows, P(None, None, ("grp", "seq")))
    return jax.shard_map(on_device, mesh=mesh, in_specs=placed, out_specs=rows, check_vma=False)
```

time: 114 us -> 49.5 us (0.43)
  the two profiles are of different devices: /device:TPU:25 before, /device:TPU:29 now
where the time goes in v1:
time: 49.5 us; the launch traced here: 49.4 us
  Pallas kernels  47.5 us (96%)
  local copies, waits for them, and re-layouts  1.88 us (4%)
    pallas_call x1, Pallas kernels, on_device(): pl.pallas_call(functools.partial(kernel, (tok, heads, width, value, bits,...  47.5 us
    unnamed x1, local copies, waits for them, and re-layouts  1.88 us

profile of v1, /device:TPU:29, one launch (start us, length us, event | category | flops | bytes accessed | tf_op | source)
XLA Modules:
  0.0 49.4 jit_solution(2259653598259424839)
XLA Ops:
  0.0 47.5 %shard_map.46 = bf16[128,2048]{1,0:T(8,128)(2,1)} custom-call(bf16[128,4096]{1,0:T(8,128)(2,1)} %q_hbm.1, bf16[128,4096]{1,0:T(8,128)(2,1)} %k_hbm.1, bf16[128,2048]{1,0:T(8,128)(2,1)} %v_hbm.1, bf16[12,32,128]{2,1,0:T(8,128)(2,1)} %lw_hbm.1), custom_call_target="tpu_custom_call" | custom-call | tf_op jit(solution)/shard_map/pallas_call | solution.py:308
  47.5 1.9 %copy.6 = bf16[128,2048]{1,0:T(8,128)(2,1)} copy(bf16[128,2048]{1,0:T(8,128)(2,1)} %shard_map.46) | data formatting | bytes 1048576

commit v2 on v1

--- a/solution.py
+++ b/solution.py
@@ -8,6 +8,7 @@
 from jax.sharding import PartitionSpec as P
 
 CHUNKS = 4
+GROUP = 4
 MESH = pl.DeviceIdType.MESH
 F32 = jnp.float32
 BF16 = jnp.bfloat16
@@ -130,59 +131,90 @@
     def forward_in(j, i):
         return remote(levels.at[j, piece(other, i)], levels.at[j, piece(other, i)], 1 + last + j, i, mate)
 
-    def sends(j):
+    def direct(i):
+        return bit(last - 2) == i % 2
+
+    def need(j, i, own_bit):
+        if j == last - 1:
+            return bit(last) == 0
+        if j == last - 2:
+            return (bit(last) == 0) | (bit(last - 1) == 0) if own_bit == i % 2 else bit(last) == 0
+        return open_above(j)
+
+    def sends(j, i):
         if j == last:
             return edge_low
-        up = bit(j) == 0
-        return up | open_above(j) if j < last - 1 else up
-
-    def receives(j):
-        up = bit(j) == 1
-        return up | open_above(j) if j < last - 1 else up
+        if j == last - 1:
+            return (bit(j) == 0) & ((bit(last) == 0) | direct(i))
+        return (bit(j) == 0) | need(j, i, 0)
+
+    def sums(j, i):
+        upper = (bit(j) == 1) & need(j, i, 1)
+        return upper if j == last - 1 else upper | ((bit(j) == 0) & need(j, i, 0))
+
+    def across(i):
+        return remote(levels.at[last - 1, piece(core, i)], levels.at[last - 1, piece(core, i)],
+                      2 * bits, i, toggled(last - 2))
+
+    crossing = (bit(last) == 1) & (bit(last - 1) == 1)
 
     for n in range(chunks):
         make_state(n)
         if n == 0:
             pl.semaphore_wait(barrier, last + (bit(last) + bit(last - 1)) % 2)
         swap(n).start()
+    for n in range(chunks):
+        make_state(chunks + n)
+    for i in range(chunks):
+        swap_in(i).wait_recv()
+        mine = piece(core, i)
+        totals[0, pl.ds(i * rows, rows), :] = own[mine, :] + levels[0, mine, :]
+
+        @pl.when(sends(1, i))
+        def _():
+            main(1, i).start()
+
+    @pl.when(core == 0)
+    def _():
+        for i in range(chunks):
+            extra(i).start()
 
     def event(j, i):
-        if j == 0:
-            make_state(chunks + i)
-
-            @pl.when(core == 0)
-            def _():
-                extra(i).start()
-
-            swap_in(i).wait_recv()
-            mine = piece(core, i)
-            totals[0, pl.ds(i * rows, rows), :] = own[mine, :] + levels[0, mine, :]
-
-            @pl.when(sends(1))
-            def _():
-                main(1, i).start()
-            return
-
-        @pl.when(receives(j))
-        def _():
-            main_in(j, i).wait_recv()
-            if j == last:
-                @pl.when(edge_high)
+        if j == last - 1:
+            @pl.when((bit(j) == 1) & ((bit(last) == 0) | direct(i)))
+            def _():
+                main_in(j, i).wait_recv()
+
+            @pl.when(crossing & direct(i))
+            def _():
+                across(i).start()
+
+            @pl.when(crossing & jnp.logical_not(direct(i)))
+            def _():
+                across(i).wait_recv()
+        else:
+            up = bit(j) == 1
+
+            @pl.when(up if j == last else up | need(j, i, 0))
+            def _():
+                main_in(j, i).wait_recv()
+        if j == last:
+            @pl.when(edge_high)
+            def _():
+                pass_on(i).start()
+        else:
+            @pl.when(sums(j, i))
+            def _():
+                part = pl.ds(i * rows, rows)
+                totals[j, part, :] = totals[j - 1, part, :] + levels[j, piece(core, i), :]
+
+                @pl.when(sends(j + 1, i))
                 def _():
-                    pass_on(i).start()
-            else:
-                @pl.when(open_above(j))
-                def _():
-                    part = pl.ds(i * rows, rows)
-                    totals[j, part, :] = totals[j - 1, part, :] + levels[j, piece(core, i), :]
-
-                    @pl.when(sends(j + 1))
-                    def _():
-                        main(j + 1, i).start()
-
-            @pl.when(bit(j) == 1)
-            def _():
-                forward(j, i).start()
+                    main(j + 1, i).start()
+
+        @pl.when(bit(j) == 1)
+        def _():
+            forward(j, i).start()
 
     def prepare():
         load_lw.wait()
@@ -197,41 +229,45 @@
         depth[...] = jnp.where(key_pos <= query_pos, level_map, local_levels)
         load_q.wait()
 
-    def local(start, stop):
-        @pl.loop(start, stop)
-        def _(n):
-            head = lax.rem(n + other * half, heads)
-            scores = lax.dot_general(k[:, cols(head, 1, width)], q[:, cols(head, 1, width)], NT,
-                                     preferred_element_type=F32)
-            level_map = depth[...]
+    def local(side, start, count):
+        group = [side * half + start + n for n in range(count)]
+        level_map = depth[...]
+        scores = [lax.dot_general(k[:, cols(head, 1, width)], q[:, cols(head, 1, width)], NT,
+                                  preferred_element_type=F32) for head in group]
+        values = [vt[state_rows(head), :] for head in group]
+        weights = []
+        for n, head in enumerate(group):
             mixing = jnp.zeros((tok, tok), F32)
             for level in range(local_levels):
                 mixing = jnp.where(level_map == level, lam[level, pl.ds(head, 1), :], mixing)
-            weight = (mixing * scores).astype(BF16)
-            acc[state_rows(head), :] = lax.dot_general(vt[state_rows(head), :], weight, NN,
-                                                       preferred_element_type=F32)
+            weights.append((mixing * scores[n]).astype(BF16))
+        results = [lax.dot_general(value_rows, weight, NN, preferred_element_type=F32)
+                   for value_rows, weight in zip(values, weights)]
+        for head, result in zip(group, results):
+            acc[state_rows(head), :] = result
 
     def cross(j, side, i):
-        @pl.loop(0, per)
-        def _(n):
-            head = first_head(side, i) + n
+        group = [first_head(side, i) + n for n in range(per)]
+        pairs = []
+        for head in group:
             part = levels[j, state_rows(head), :]
             upper = part.astype(BF16)
             lower = (part - upper.astype(F32)).astype(BF16)
-            query = q[:, cols(head, 1, width)]
-            product = lax.dot_general(jnp.concatenate([upper, lower], axis=1),
-                                      jnp.concatenate([query, query], axis=1), NT,
-                                      preferred_element_type=F32)
-            acc[state_rows(head), :] += lam[local_levels + j, pl.ds(head, 1), :] * product
-
-    def cross_level(j):
+            pairs.append(jnp.concatenate([upper, lower], axis=1))
+        queries = [q[:, cols(head, 1, width)] for head in group]
+        products = [lax.dot_general(pair, jnp.concatenate([query, query], axis=1), NT,
+                                    preferred_element_type=F32) for pair, query in zip(pairs, queries)]
+        results = [acc[state_rows(head), :] + lam[local_levels + j, pl.ds(head, 1), :] * product
+                   for head, product in zip(group, products)]
+        for head, result in zip(group, results):
+            acc[state_rows(head), :] = result
+
+    def cross_piece(j, side, i):
         @pl.when(bit(j) == 1)
         def _():
-            for i in range(chunks):
-                cross(j, core, i)
-            for i in range(chunks):
+            if side is other:
                 (extra_in(i) if j == 0 else forward_in(j, i)).wait_recv()
-                cross(j, other, i)
+            cross(j, side, i)
 
     def out_copy(side, i):
         n = i if side is core else chunks + i
@@ -244,32 +280,37 @@
             out[:, cols(head + p, 2, value)] = acc[state_rows(head + p, 2), :].T.astype(BF16)
         out_copy(side, i).start()
 
-    steps = chunks + bits - 1
-    share = -(-heads // (steps - 2))
-    done = 0
-    pending = list(range(last))
-    for d in range(steps):
-        for j in reversed(range(bits)):
-            if 0 <= d - j < chunks:
-                event(j, d - j)
-        if d == 0:
-            prepare()
-        stop = min(heads, done + share)
-        if stop > done:
-            local(done, stop)
-        done = stop
-        if done == heads and d >= steps - last and pending:
-            cross_level(pending.pop(0))
-    for j in pending:
-        cross_level(j)
-    for side, receive in ((core, None), (other, forward_in)):
-        for i in range(chunks):
-            @pl.when(bit(last) == 1)
-            def _():
-                if receive is not None:
-                    receive(last, i).wait_recv()
-                cross(last, side, i)
-            finish(side, i)
+    prepare()
+    events = sorted(((j, i) for j in range(1, bits) for i in range(chunks)), key=lambda e: (e[0] + e[1], e[0]))
+    at = {e: n for n, e in enumerate(events)}
+    group = min(GROUP, half)
+    work = [(-1, 2, functools.partial(local, side, start, group))
+            for side in (other, core) for start in range(0, half, group)]
+    for j in range(last):
+        for side in (core, other):
+            for i in range(chunks):
+                ready = at[j, min(i + (side is other), chunks - 1)] if j else -1
+                work.append((ready, 1 / chunks * 4, functools.partial(cross_piece, j, side, i)))
+    budget = sum(w[1] for w in work) / (len(events) - 1)
+    spent = 0.0
+
+    def spend(n, limit):
+        nonlocal spent
+        while work and work[0][0] <= n and spent < limit:
+            _, weight, run = work.pop(0)
+            run()
+            spent += weight
+
+    spend(-1, budget)
+    for n, e in enumerate(events):
+        event(*e)
+        spend(n, budget * (n + 2))
+    spend(len(events), float("inf"))
+    for i in range(chunks):
+        cross_piece(last, core, i)
+        finish(core, i)
+        cross_piece(last, other, i)
+        finish(other, i)
 
     for i in range(chunks):
         swap(i).wait_send()
@@ -279,7 +320,7 @@
             extra(i).wait_send()
 
         for j in range(1, bits):
-            @pl.when(sends(j))
+            @pl.when(sends(j, i))
             def _():
                 main(j, i).wait_send()
 
@@ -290,6 +331,10 @@
         @pl.when(edge_high)
         def _():
             pass_on(i).wait_send()
+
+        @pl.when(crossing & direct(i))
+        def _():
+            across(i).wait_send()
 
         out_copy(core, i).wait()
         out_copy(other, i).wait()

time: 49.5 us -> 41.3 us (0.83)
  the two profiles are of different devices: /device:TPU:29 before, /device:TPU:25 now
where the time goes in v2:
time: 41.3 us; the launch traced here: 41.1 us
  Pallas kernels  39.2 us (95%)
  local copies, waits for them, and re-layouts  1.88 us (5%)
    pallas_call x1, Pallas kernels, on_device(): pl.pallas_call(functools.partial(kernel, (tok, heads, width, value, bits,...  39.2 us
    unnamed x1, local copies, waits for them, and re-layouts  1.88 us

profile of v2, /device:TPU:25, one launch (start us, length us, event | category | flops | bytes accessed | tf_op | source)
XLA Modules:
  0.0 41.1 jit_solution(2807317431000048351)
XLA Ops:
  0.0 39.2 %shard_map.46 = bf16[128,2048]{1,0:T(8,128)(2,1)} custom-call(bf16[128,4096]{1,0:T(8,128)(2,1)} %q_hbm.1, bf16[128,4096]{1,0:T(8,128)(2,1)} %k_hbm.1, bf16[128,2048]{1,0:T(8,128)(2,1)} %v_hbm.1, bf16[12,32,128]{2,1,0:T(8,128)(2,1)} %lw_hbm.1), custom_call_target="tpu_custom_call" | custom-call | tf_op jit(solution)/shard_map/pallas_call | solution.py:353
  39.2 1.9 %copy.6 = bf16[128,2048]{1,0:T(8,128)(2,1)} copy(bf16[128,2048]{1,0:T(8,128)(2,1)} %shard_map.46) | data formatting | bytes 1048576

commit v3 on v2

--- a/solution.py
+++ b/solution.py
@@ -291,6 +291,13 @@
             for i in range(chunks):
                 ready = at[j, min(i + (side is other), chunks - 1)] if j else -1
                 work.append((ready, 1 / chunks * 4, functools.partial(cross_piece, j, side, i)))
+    def close(side, i):
+        cross_piece(last, side, i)
+        finish(side, i)
+
+    ends = [(at[last, min(i + (side is other), chunks - 1)], 0, functools.partial(close, side, i))
+            for i in range(chunks) for side in (core, other)]
+    work += sorted(ends, key=lambda w: w[0])
     budget = sum(w[1] for w in work) / (len(events) - 1)
     spent = 0.0
 
@@ -306,12 +313,6 @@
         event(*e)
         spend(n, budget * (n + 2))
     spend(len(events), float("inf"))
-    for i in range(chunks):
-        cross_piece(last, core, i)
-        finish(core, i)
-        cross_piece(last, other, i)
-        finish(other, i)
-
     for i in range(chunks):
         swap(i).wait_send()
 

time: 41.3 us -> 41.5 us (level)
  no operation moved by 1% of the time
where the time goes in v3:
time: 41.5 us; the launch traced here: 41.4 us
  Pallas kernels  39.5 us (95%)
  local copies, waits for them, and re-layouts  1.88 us (5%)
    pallas_call x1, Pallas kernels, on_device(): pl.pallas_call(functools.partial(kernel, (tok, heads, width, value, bits,...  39.5 us
    unnamed x1, local copies, waits for them, and re-layouts  1.88 us

profile of v3, /device:TPU:25, one launch (start us, length us, event | category | flops | bytes accessed | tf_op | source)
XLA Modules:
  0.0 41.4 jit_solution(12774129123878750917)
XLA Ops:
  0.0 39.5 %shard_map.46 = bf16[128,2048]{1,0:T(8,128)(2,1)} custom-call(bf16[128,4096]{1,0:T(8,128)(2,1)} %q_hbm.1, bf16[128,4096]{1,0:T(8,128)(2,1)} %k_hbm.1, bf16[128,2048]{1,0:T(8,128)(2,1)} %v_hbm.1, bf16[12,32,128]{2,1,0:T(8,128)(2,1)} %lw_hbm.1), custom_call_target="tpu_custom_call" | custom-call | tf_op jit(solution)/shard_map/pallas_call | solution.py:354
  39.5 1.9 %copy.6 = bf16[128,2048]{1,0:T(8,128)(2,1)} copy(bf16[128,2048]{1,0:T(8,128)(2,1)} %shard_map.46) | data formatting | bytes 1048576
